TPU v7x, 32 devices: a whole 2x2x4 slice. The times are simulated.
32 devices in a mesh: groups: 2 (over x), tm: 8 (over z, y), space: 2 (over core).
Axes of the slice: x: 2, y: 2, z: 4, core: 2. Of those that a mesh axis runs over, the one named last changes fastest.
Arguments:
- query_pre: bfloat16 [16, 8, 32, 2240], P(('groups', 'tm'), 'space'), parts along dimension 0, may hold values from -6 to 6
- key_pre: bfloat16 [16, 8, 32, 2240], P(('groups', 'tm'), 'space'), parts along dimension 0, may hold values from -6 to 6
- value_pre: bfloat16 [16, 8, 32, 2240], P(('groups', 'tm'), 'space'), parts along dimension 0, may hold values from -8 to 8
- grad_out: bfloat16 [16, 8, 32, 2240], P(('groups', 'tm'), 'space'), parts along dimension 0, may hold values from -96 to 96
- conv_taps: float32 [3, 3, 2240], replicated, may hold values from -4 to 4
Outputs:
- attended: bfloat16 [16, 8, 32, 2240], P(('groups', 'tm'), 'space'), parts along dimension 0
- query_grad: bfloat16 [16, 8, 32, 2240], P(('groups', 'tm'), 'space'), parts along dimension 0
- key_grad: bfloat16 [16, 8, 32, 2240], P(('groups', 'tm'), 'space'), parts along dimension 0
- value_grad: bfloat16 [16, 8, 32, 2240], P(('groups', 'tm'), 'space'), parts along dimension 0
- taps_grad: float32 [6, 3, 2240], P('groups'), parts along dimension 0
There are 2 independent parts, one for each index of `groups`. A program takes and returns all parts, laid end to end along the dimension named above; an argument that names none is the same for every part. Nothing has to cross between parts.
All inputs are finite; a program needn't handle non-finite values.
Results may differ from a plain program's by a relative error of at most 0.013.
Values may be sent and summed in bfloat16 or wider, within the bound.
A program may use at most 128 MiB of HBM per device.

v0:
```python
import jax
import jax.numpy as jnp
from jax import lax
from jax.sharding import PartitionSpec as P

HEADS = 20
HEAD_DIM = 112


def extended(block, sides, width):
    for axis, dim in sides:
        count = lax.axis_size(axis)
        forward = [(i, i + 1) for i in range(count - 1)]
        backward = [(target, source) for source, target in forward]
        low = lax.ppermute(
            lax.slice_in_dim(block, block.shape[dim] - width, None, axis=dim), axis, forward
        )
        high = lax.ppermute(lax.slice_in_dim(block, 0, width, axis=dim), axis, backward)
        block = jnp.concatenate([low, block, high], axis=dim)
    return block


def carried_in(part, axis, combine, identity):
    place = lax.axis_index(axis)
    gathered = jax.tree.map(lambda a: lax.all_gather(a, axis), part)
    state = jax.tree.map(lambda a, e: jnp.zeros_like(a) + jnp.asarray(e, a.dtype), part, identity)

    def one(turn, state):
        return combine(
            state, jax.tree.map(lambda a: lax.dynamic_index_in_dim(a, turn, 0, False), gathered)
        )

    return lax.fori_loop(0, place, one, state)


def carried_in_2(x, axis, join, neutral):
    count = lax.axis_size(axis)
    place = lax.axis_index(axis)
    ahead = count - 1 - place
    gathered = jax.tree.map(
        lambda a, kind: lax.all_gather(a.astype(kind), axis), x, (jnp.bfloat16, jnp.bfloat16)
    )
    state = jax.tree.map(lambda a, e: jnp.zeros_like(a) + jnp.asarray(e, a.dtype), x, neutral)

    def one(turn, state):
        source = count - 1 - turn
        return join(
            state,
            jax.tree.map(
                lambda a, own: lax.dynamic_index_in_dim(a, source, 0, False).astype(own.dtype),
                gathered,
                x,
            ),
        )

    return lax.fori_loop(0, ahead, one, state)


def mix_rows(padded, conv_taps, row_count, col_count, flipped):
    summed = jnp.zeros(padded.shape[:1] + (row_count, col_count, padded.shape[3]), jnp.float32)
    for row_off in range(3):
        for col_off in range(3):
            if flipped:
                window = padded[
                    :, 2 - row_off : 2 - row_off + row_count, 2 - col_off : 2 - col_off + col_count
                ]
            else:
                window = padded[:, row_off : row_off + row_count, col_off : col_off + col_count]
            summed = summed + conv_taps[row_off, col_off] * window
    return summed


def add_pair(earlier, later):
    return (earlier[0] + later[0], earlier[1] + later[1])


def shards(query_pre, key_pre, value_pre, grad_out, conv_taps):
    frame_count, row_count, col_count, model_width = value_pre.shape
    head_count = HEADS
    head_size = HEAD_DIM
    token_count = frame_count * row_count * col_count
    split = (token_count, head_count, head_size)
    highest = lax.Precision.HIGHEST
    value_rows, grad_band = (
        extended(value_pre, (("space", 1),), 1),
        extended(grad_out, (("space", 1),), 1),
    )
    value_pad = jnp.pad(value_rows, ((0, 0), (0, 0), (1, 1), (0, 0)))
    local = mix_rows(value_pad, conv_taps, row_count, col_count, False)
    queries = jnp.maximum(query_pre, 0).reshape(split)
    keys = jnp.maximum(key_pre, 0).reshape(split)
    values = value_pre.reshape(split)
    partial_value = jnp.einsum("the,thd->hed", keys, values, preferred_element_type=jnp.float32)
    key_sum = jnp.sum(keys, axis=0, dtype=jnp.float32)
    half_state, half_sum = (
        lax.psum_scatter(partial_value, "space", scatter_dimension=0, tiled=True),
        lax.psum_scatter(key_sum, "space", scatter_dimension=0, tiled=True),
    )
    before = carried_in(
        (half_state, half_sum),
        "tm",
        add_pair,
        (jnp.zeros_like(half_state), jnp.zeros_like(half_sum)),
    )
    kv_state, key_total = (
        lax.all_gather(before[0] + half_state, "space", axis=0, tiled=True),
        lax.all_gather(before[1] + half_sum, "space", axis=0, tiled=True),
    )
    query_f32 = queries.astype(jnp.float32)
    numerator = jnp.einsum("the,hed->thd", query_f32, kv_state, precision=highest)
    denominator = jnp.einsum("the,he->th", query_f32, key_total, precision=highest) + 1.0
    output_f32 = numerator / denominator[..., None]
    attended = (output_f32.reshape(value_pre.shape) + local).astype(jnp.bfloat16)
    cotangent = grad_out.astype(jnp.float32).reshape(split)
    grad_num = cotangent / denominator[..., None]
    grad_den = -jnp.sum(cotangent * output_f32, axis=-1) / denominator
    grad_query = (
        jnp.einsum("thd,hed->the", grad_num, kv_state, precision=highest)
        + grad_den[..., None] * key_total[None]
    )
    grad_partial = jnp.einsum("the,thd->hed", query_f32, grad_num, precision=highest)
    grad_keysum = jnp.einsum("th,the->he", grad_den, query_f32, precision=highest)
    half_grad, half_keysum = (
        lax.psum_scatter(grad_partial, "space", scatter_dimension=0, tiled=True),
        lax.psum_scatter(grad_keysum, "space", scatter_dimension=0, tiled=True),
    )
    after = carried_in_2(
        (half_grad, half_keysum),
        "tm",
        add_pair,
        (jnp.zeros_like(half_grad), jnp.zeros_like(half_keysum)),
    )
    grad_state, grad_total = (
        lax.all_gather(
            (after[0] + half_grad).astype(jnp.bfloat16), "space", axis=0, tiled=True
        ).astype(jnp.float32),
        lax.all_gather(
            (after[1] + half_keysum).astype(jnp.bfloat16), "space", axis=0, tiled=True
        ).astype(jnp.float32),
    )
    grad_key = (
        jnp.einsum("thd,hed->the", values.astype(jnp.float32), grad_state, precision=highest)
        + grad_total[None]
    )
    grad_mixed = jnp.einsum(
        "the,hed->thd", keys.astype(jnp.float32), grad_state, precision=highest
    ).reshape(value_pre.shape)
    query_grad = jnp.where(query_pre > 0, grad_query.reshape(value_pre.shape), 0.0).astype(
        jnp.bfloat16
    )
    key_grad = jnp.where(key_pre > 0, grad_key.reshape(value_pre.shape), 0.0).astype(jnp.bfloat16)
    grad_pad = jnp.pad(grad_band, ((0, 0), (0, 0), (1, 1), (0, 0)))
    value_grad = (grad_mixed + mix_rows(grad_pad, conv_taps, row_count, col_count, True)).astype(
        jnp.bfloat16
    )
    cotangent_full = grad_out.astype(jnp.float32)
    tap_rows = []
    for row_off in range(3):
        tap_cols = []
        for col_off in range(3):
            window = value_pad[:, row_off : row_off + row_count, col_off : col_off + col_count]
            tap_cols.append(jnp.sum(cotangent_full * window, axis=(0, 1, 2)))
        tap_rows.append(jnp.stack(tap_cols))
    taps_grad = lax.psum(jnp.stack(tap_rows), ("tm", "space"))
    return (attended, query_grad, key_grad, value_grad, taps_grad)


def solution(mesh):
    return jax.shard_map(
        shards,
        mesh=mesh,
        in_specs=(
            P(("groups", "tm"), "space", None, None),
            P(("groups", "tm"), "space", None, None),
            P(("groups", "tm"), "space", None, None),
            P(("groups", "tm"), "space", None, None),
            P(),
        ),
        out_specs=(
            P(("groups", "tm"), "space", None, None),
            P(("groups", "tm"), "space", None, None),
            P(("groups", "tm"), "space", None, None),
            P(("groups", "tm"), "space", None, None),
            P("groups", None, None),
        ),
        check_vma=False,
    )
```

profile of v0, /device:TPU:8, one launch (start us, length us, event | category | flops | bytes accessed | tf_op | source)
XLA Modules:
  0.0 254.5 jit_solution(9472925568814212947)
XLA Ops:
  8.0 1.1 broadcast_maximum_fusion.1
  11.8 1.5 fusion.43
  13.3 10.1 %reduce-scatter.7.cloned.1.call-done = f32[10,112,112]{2,1,0:T(8,128)} async-done(((f32[20,112,112]{2,1,0:T(8,128)}), f32[10,112,112]{2,1,0:T(8,128)}) %reduce-scatter.7.cloned.1.call-update) | async-done | bytes 501776 | tf_op jit(solution)/shard_map/reduce_scatter | solution.py:96
  23.7 2.7 %fusion = f32[16,112]{1,0:T(8,128)S(1)} fusion(f32[20,112]{1,0:T(8,128)S(1)} %reduce_sum.102), kind=kCustom, calls=%all-reduce-scatter | all-reduce-scatter fusion | flops 3585 | bytes 16640
  26.4 2.2 collective-permute-start.4
  30.3 1.5 copy.42
  33.0 2.0 reshape.72
  35.7 28.8 %all-gather.4 = f32[8,10,112]{2,1,0:T(8,128)S(1)} all-gather(f32[1,10,112]{2,1,0:T(8,128)S(1)} %fusion.37), channel_id=3, replica_groups=mesh['groups'=2,'tm'=8,'space'=2] {'tm'}, dimensions={0}, use_global_device_ids=true | all-gather | bytes 40320 | tf_op jit(solution)/shard_map/all_gather | solution.py:25
  64.5 39.8 %all-gather.11.cloned.1.call-done = f32[80,112,112]{2,1,0:T(8,128)} async-done(((f32[10,112,112]{2,1,0:T(8,128)}), f32[80,112,112]{2,1,0:T(8,128)}) %all-gather.11.cloned.1.call-update) | async-done | bytes 4014096 | tf_op jit(solution)/shard_map/all_gather | solution.py:25
  104.3 2.5 while.26
  104.4 1.3 bitcast_add_fusion.5
  105.7 1.2 bitcast_add_fusion.5
  107.6 1.8 all-gather.5
  110.0 2.4 fusion.33
  112.5 13.9 %reduce-scatter.9.cloned.1.call-done = f32[10,112,112]{2,1,0:T(8,128)} async-done(((f32[20,112,112]{2,1,0:T(8,128)}), f32[10,112,112]{2,1,0:T(8,128)}) %reduce-scatter.9.cloned.1.call-update) | async-done | bytes 501776 | tf_op jit(solution)/shard_map/reduce_scatter | solution.py:124
  126.4 1.8 convert_element_type.134
  128.3 1.3 collective-permute-start.1
  129.6 3.0 %collective-permute-start = (bf16[1,1,32,2240]{3,2,1,0:T(8,128)(2,1)S(1)}, bf16[1,1,32,2240]{3,2,1,0:T(8,128)(2,1)S(1)}, u32[]{:S(2)}, u32[]{:S(2)}) collective-permute-start(bf16[1,1,32,2240]{3,2,1,0:T(8,128)(2,1)S(1)} %get-tuple-element.171), channel_id=1, source_target_pairs={{0,1},{2,3},{4,5},{6,7},{8,9},{10,11},{12,13},{14,15},{16,17},{18,... | collective-permute-start | bytes 430088 | tf_op jit(solution)/shard_map/ppermute | solution.py:15
  133.4 1.3 collective-permute-start.3
  134.7 3.7 %collective-permute-start.2 = (bf16[1,1,32,2240]{3,2,1,0:T(8,128)(2,1)}, bf16[1,1,32,2240]{3,2,1,0:T(8,128)(2,1)}, u32[]{:S(2)}, u32[]{:S(2)}) collective-permute-start(bf16[1,1,32,2240]{3,2,1,0:T(8,128)(2,1)} %get-tuple-element.169), channel_id=1, source_target_pairs={{0,1},{2,3},{4,5},{6,7},{8,9},{10,11},{12,13},{14,15},{16,17},{18,... | collective-permute-start | bytes 430088 | tf_op jit(solution)/shard_map/ppermute | solution.py:15
  139.5 1.1 fusion.23
  142.3 1.5 select_maximum_fusion
  144.4 1.1 add.145
  145.5 2.9 %all_gather.40 = f32[20,112,112]{2,1,0:T(8,128)S(1)} all-gather(f32[10,112,112]{2,1,0:T(8,128)S(1)} %add.145), channel_id=1, replica_groups=mesh['groups'=2,'tm'=8,'space'=2] {'space'}, dimensions={0}, use_global_device_ids=true | all-gather | bytes 1505280 | tf_op jit(solution)/shard_map/all_gather | solution.py:106
  148.5 2.7 %multiply_reduce_fusion = (f32[128,20]{0,1:T(8,128)}, f32[128,20,112]{0,2,1:T(8,128)}) fusion(f32[128,20,112]{0,2,1:T(8,128)S(1)} %copy-done.18, f32[128,20]{0,1:T(8,128)S(1)} %copy-done.37, f32[20,112,112]{2,1,0:T(8,128)S(1)} %all_gather.40, bf16[128,20,112]{0,2,1:T(8,128)(2,1)S(1)} %copy-done.10), kind=kOutput, calls=%fused_computation.62 | convolution fusion | flops 386209280 | bytes 3891200 | tf_op jit(solution)/shard_map/the,hed->thd/dot_general | solution.py:110
  151.2 2.9 %copy.41 = f32[128,20,112]{2,1,0:T(8,128)} copy(f32[128,20,112]{0,2,1:T(8,128)} %get-tuple-element.174) | data formatting | bytes 2293760 | tf_op jit(solution)/shard_map/div | solution.py:112
  154.2 2.7 %reshape.73 = f32[1,4,32,2240]{3,2,1,0:T(8,128)} reshape(f32[128,20,112]{2,1,0:T(8,128)} %copy.41) | data formatting | bytes 2293760 | tf_op jit(solution)/shard_map/reshape | solution.py:113
  158.6 2.7 %fusion.1 = f32[16,112]{1,0:T(8,128)S(1)} fusion(f32[20,112]{1,0:T(8,128)S(1)} %bitcast.88), kind=kCustom, calls=%all-reduce-scatter.1 | all-reduce-scatter fusion | flops 3585 | bytes 16640
  161.3 2.2 collective-permute-start.5
  163.6 3.3 %fusion.15 = bf16[1,4,32,2240]{3,2,1,0:T(8,128)(2,1)} fusion(f32[1,4,32,2240]{3,2,1,0:T(8,128)} %reshape.73, bf16[1,4,32,2240]{3,2,1,0:T(8,128)(2,1)S(1)} %copy-done, bf16[1,1,32,2240]{3,2,1,0:T(8,128)(2,1)S(1)} %collective-permute-done.1, bf16[1,1,32,2240]{3,2,1,0:T(8,128)(2,1)} %copy-done.14, f32[2240]{0:T(1024)} %get-tuple-element.143, ...), kind=kLoop, calls=%fused_computation.42 | loop fusion | flops 8601600 | bytes 6101760 | tf_op jit(solution)/shard_map/convert_element_type | solution.py:113
  166.9 1.4 fusion.5
  168.8 1.4 reshape.75
  170.3 28.0 %all-gather.6 = bf16[8,10,112]{2,1,0:T(8,128)(2,1)S(1)} all-gather(bf16[1,10,112]{2,1,0:T(8,128)(2,1)S(1)} %fusion.39), channel_id=5, replica_groups=mesh['groups'=2,'tm'=8,'space'=2] {'tm'}, dimensions={0}, use_global_device_ids=true | all-gather | bytes 20160 | tf_op jit(solution)/shard_map/all_gather | solution.py:41
  198.4 5.6 %while.27 = (s32[]{:T(128)}, f32[10,112,112]{2,1,0:T(8,128)S(1)}, f32[10,112]{1,0:T(8,128)S(1)}, s32[]{:T(128)}, bf16[8,10,112,112]{3,2,1,0:T(8,128)(2,1)}, /*in...) while((s32[]{:T(128)}, f32[10,112,112]{2,1,0:T(8,128)S(1)}, ...), condition=%wide.region_9.10_spmd, body=%wide.region_8.9_spmd.sunk | while | flops 253126 | bytes 1265763 | solution.py:56
  198.4 1.1 convert_add_fusion.4
  199.6 1.1 convert_add_fusion.4
  204.1 2.3 all_gather.46
  206.5 1.9 all-gather.7
  208.5 1.4 convolution_bitcast_fusion
  209.8 1.3 fusion.3
  211.1 1.6 copy.47
  212.7 1.4 reshape.76
  214.1 1.6 copy.50
  215.7 1.9 reshape.77
  217.7 2.8 %select_convert_fusion = (bf16[1,4,32,2240]{3,2,1,0:T(8,128)(2,1)}, bf16[1,4,32,2240]{3,2,1,0:T(8,128)(2,1)}) fusion(bf16[1,4,32,2240]{3,2,1,0:T(8,128)(2,1)} %reshape.76, bf16[1,4,32,2240]{3,2,1,0:T(8,128)(2,1)S(1)} %copy-done.4, bf16[1,4,32,2240]{3,2,1,0:T(8,128)(2,1)} %reshape.75, bf16[1,4,32,2240]{3,2,1,0:T(8,128)(2,1)} %param.9), kind=kLoop, calls=%fused_computation.59 | loop fusion | flops 2007040 | bytes 3440640 | tf_op jit(solution)/shard_map/convert_element_type | solution.py:151
  220.6 2.7 %fusion.22 = bf16[1,4,32,2240]{3,2,1,0:T(8,128)(2,1)} fusion(f32[1,4,32,2240]{3,2,1,0:T(8,128)S(1)} %reshape.77, bf16[1,4,32,2240]{3,2,1,0:T(8,128)(2,1)S(1)} %copy-done.2, bf16[1,6,34,2240]{3,2,1,0:T(8,128)(2,1)S(1)} %select_maximum_fusion, bf16[1,1,32,2240]{3,2,1,0:T(8,128)(2,1)} %collective-permute-done.2, bf16[1,1,32,2240]{3,2,1,0:T(8,128)(2,1)S(1)} %copy-done.21, ...), kind=kLoop, calls=%fused_computation.49 | loop fusion | flops 8601600 | bytes 6101760 | tf_op jit(solution)/shard_map/convert_element_type | solution.py:153
  223.3 22.5 %all-reduce.8.cloned.1.call-done = f32[3,3,2240]{2,1,0:T(4,128)} async-done(((f32[3,3,2240]{2,1,0:T(4,128)}), f32[3,3,2240]{2,1,0:T(4,128)}) %all-reduce.8.cloned.1.call-update) | async-done | bytes 80656 | tf_op jit(solution)/shard_map/psum | solution.py:164
  245.8 1.6 copy.83
  (155 shorter events, 17.1 us)
Async XLA Ops:
  8.0 15.4 %reduce-scatter.7.cloned.1.call-start = ((), (), s32[]{:S(2)}) async-start(), calls=%async_computation.2 | async-start | bytes 1720320 | tf_op jit(solution)/shard_map/reduce_scatter | solution.py:96
  9.2 1.3 copy-start
  11.8 1.5 copy-start.7
  13.3 10.3 %copy-start.3 = (bf16[1,4,32,2240]{3,2,1,0:T(8,128)(2,1)S(1)}, bf16[1,4,32,2240]{3,2,1,0:T(8,128)(2,1)}, u32[]{:S(2)}) copy-start(bf16[1,4,32,2240]{3,2,1,0:T(8,128)(2,1)} %param.10) | copy-start | bytes 1720324
  13.3 15.4 %copy-start.12 = (bf16[1,4,32,2240]{3,2,1,0:T(8,128)(2,1)S(1)}, bf16[1,4,32,2240]{3,2,1,0:T(8,128)(2,1)}, u32[]{:S(2)}) copy-start(bf16[1,4,32,2240]{3,2,1,0:T(8,128)(2,1)} %param.9) | copy-start | bytes 1720324
  13.3 91.0 %all-gather.11.cloned.1.call-start = ((), (), s32[]{:S(2)}) async-start(), calls=%async_computation.5 | async-start | bytes 5160960 | tf_op jit(solution)/shard_map/all_gather | solution.py:25
  23.4 6.1 %copy-start.1 = (bf16[1,4,32,2240]{3,2,1,0:T(8,128)(2,1)S(1)}, bf16[1,4,32,2240]{3,2,1,0:T(8,128)(2,1)}, u32[]{:S(2)}) copy-start(bf16[1,4,32,2240]{3,2,1,0:T(8,128)(2,1)} %param.12) | copy-start | bytes 1720324
  23.5 102.9 %reduce-scatter.9.cloned.1.call-start = ((), (), s32[]{:S(2)}) async-start(), calls=%async_computation.3 | async-start | bytes 1720320 | tf_op jit(solution)/shard_map/reduce_scatter | solution.py:124
  26.4 9.1 %collective-permute-start.4 = (f32[6,112]{1,0:T(8,128)S(1)}, f32[6,112]{1,0:T(8,128)S(1)}, u32[]{:S(2)}, u32[]{:S(2)}) collective-permute-start(f32[6,112]{1,0:T(8,128)S(1)} %slice.158), channel_id=1, source_target_pairs={{0,1},{2,3},{4,5},{6,7},{8,9},{10,11},{12,13},{14,15},{16,17},{18,... | collective-permute-start | bytes 8072
  30.3 1.5 copy-start.39
  35.5 74.5 %copy-start.9 = (bf16[128,20,112]{0,2,1:T(8,128)(2,1)}, bf16[128,20,112]{0,2,1:T(8,128)(2,1)S(1)}, u32[]{:S(2)}) copy-start(bf16[128,20,112]{0,2,1:T(8,128)(2,1)S(1)} %copy.40) | copy-start | bytes 1720324
  35.7 68.6 %copy-start.31 = (f32[22,112]{1,0:T(8,128)}, f32[22,112]{1,0:T(8,128)S(1)}, u32[]{:S(2)}) copy-start(f32[22,112]{1,0:T(8,128)S(1)} %concatenate.24) | copy-start | bytes 29572
  104.3 5.7 %copy-start.17 = (f32[128,20,112]{0,2,1:T(8,128)S(1)}, f32[128,20,112]{0,2,1:T(8,128)}, u32[]{:S(2)}) copy-start(f32[128,20,112]{0,2,1:T(8,128)} %copy.42) | copy-start | bytes 3440644
  110.0 2.4 copy-start.30
  110.0 2.4 copy-start.36
  112.4 26.0 %copy-start.32 = (f32[3,3,2240]{2,1,0:T(4,128)S(1)}, f32[3,3,2240]{2,1,0:T(4,128)}, u32[]{:S(2)}) copy-start(f32[3,3,2240]{2,1,0:T(4,128)} %param.13) | copy-start | bytes 241924
  112.4 85.9 %all-gather.13.cloned.1.call-start = ((), (), s32[]{:S(2)}) async-start(), calls=%async_computation.6 | async-start | bytes 2580480 | tf_op jit(solution)/shard_map/all_gather | solution.py:41
  128.2 117.6 %all-reduce.8.cloned.1.call-start = ((), (), s32[]{:S(2)}) async-start(), calls=%async_computation.4 | async-start | bytes 221184 | tf_op jit(solution)/shard_map/psum | solution.py:164
  128.3 10.9 %collective-permute-start.1 = (bf16[1,1,32,2240]{3,2,1,0:T(8,128)(2,1)S(1)}, bf16[1,1,32,2240]{3,2,1,0:T(8,128)(2,1)S(1)}, u32[]{:S(2)}, u32[]{:S(2)}) collective-permute-start(bf16[1,1,32,2240]{3,2,1,0:T(8,128)(2,1)S(1)} %get-tuple-element.172), channel_id=1, source_target_pairs={{1,0},{3,2},{5,4},{7,6},{9,8},{11,10},{13,12},{15,14},{17,16},{19,... | collective-permute-start | bytes 430088 | tf_op jit(solution)/shard_map/ppermute | solution.py:18
  129.6 9.6 %collective-permute-start = (bf16[1,1,32,2240]{3,2,1,0:T(8,128)(2,1)S(1)}, bf16[1,1,32,2240]{3,2,1,0:T(8,128)(2,1)S(1)}, u32[]{:S(2)}, u32[]{:S(2)}) collective-permute-start(bf16[1,1,32,2240]{3,2,1,0:T(8,128)(2,1)S(1)} %get-tuple-element.171), channel_id=1, source_target_pairs={{0,1},{2,3},{4,5},{6,7},{8,9},{10,11},{12,13},{14,15},{16,17},{18,... | collective-permute-start | bytes 430088 | tf_op jit(solution)/shard_map/ppermute | solution.py:15
  133.4 8.2 %collective-permute-start.3 = (bf16[1,1,32,2240]{3,2,1,0:T(8,128)(2,1)}, bf16[1,1,32,2240]{3,2,1,0:T(8,128)(2,1)S(1)}, u32[]{:S(2)}, u32[]{:S(2)}) collective-permute-start(bf16[1,1,32,2240]{3,2,1,0:T(8,128)(2,1)} %get-tuple-element.170), channel_id=1, source_target_pairs={{1,0},{3,2},{5,4},{7,6},{9,8},{11,10},{13,12},{15,14},{17,16},{19,... | collective-permute-start | bytes 430088 | tf_op jit(solution)/shard_map/ppermute | solution.py:18
  134.7 7.6 %collective-permute-start.2 = (bf16[1,1,32,2240]{3,2,1,0:T(8,128)(2,1)}, bf16[1,1,32,2240]{3,2,1,0:T(8,128)(2,1)}, u32[]{:S(2)}, u32[]{:S(2)}) collective-permute-start(bf16[1,1,32,2240]{3,2,1,0:T(8,128)(2,1)} %get-tuple-element.169), channel_id=1, source_target_pairs={{0,1},{2,3},{4,5},{6,7},{8,9},{10,11},{12,13},{14,15},{16,17},{18,... | collective-permute-start | bytes 430088 | tf_op jit(solution)/shard_map/ppermute | solution.py:15
  139.2 1.5 copy-start.14
  144.4 4.1 %copy-start.37 = (f32[128,20]{0,1:T(8,128)S(1)}, f32[128,20]{0,1:T(8,128)}, u32[]{:S(2)}) copy-start(f32[128,20]{0,1:T(8,128)} %copy-done.36) | copy-start | bytes 30724
  145.5 3.0 %copy-start.10 = (bf16[128,20,112]{0,2,1:T(8,128)(2,1)S(1)}, bf16[128,20,112]{0,2,1:T(8,128)(2,1)}, u32[]{:S(2)}) copy-start(bf16[128,20,112]{0,2,1:T(8,128)(2,1)} %copy-done.9) | copy-start | bytes 1720324
  145.5 3.0 %copy-start.18 = (f32[128,20,112]{0,2,1:T(8,128)S(1)}, f32[128,20,112]{0,2,1:T(8,128)}, u32[]{:S(2)}) copy-start(f32[128,20,112]{0,2,1:T(8,128)} %copy.42) | copy-start | bytes 3440644
  148.5 2.7 %copy-start.15 = (f32[20,112,112]{2,1,0:T(8,128)}, f32[20,112,112]{2,1,0:T(8,128)S(1)}, u32[]{:S(2)}) copy-start(f32[20,112,112]{2,1,0:T(8,128)S(1)} %all_gather.40) | copy-start | bytes 3010564
  154.1 9.4 %copy-start.22 = (f32[2240]{0:T(1024)S(1)}, f32[2240]{0:T(1024)}, u32[]{:S(2)}) copy-start(f32[2240]{0:T(1024)} %get-tuple-element.137) | copy-start | bytes 26884
  161.3 8.9 %collective-permute-start.5 = (f32[6,112]{1,0:T(8,128)S(1)}, f32[6,112]{1,0:T(8,128)S(1)}, u32[]{:S(2)}, u32[]{:S(2)}) collective-permute-start(f32[6,112]{1,0:T(8,128)S(1)} %slice.159), channel_id=1, source_target_pairs={{0,1},{2,3},{4,5},{6,7},{8,9},{10,11},{12,13},{14,15},{16,17},{18,... | collective-permute-start | bytes 8072
  163.5 3.4 %copy-start.16 = (f32[20,112,112]{2,1,0:T(8,128)S(1)}, f32[20,112,112]{2,1,0:T(8,128)}, u32[]{:S(2)}) copy-start(f32[20,112,112]{2,1,0:T(8,128)} %copy-done.15) | copy-start | bytes 3010564
  163.5 3.4 %copy-start.19 = (f32[128,20,112]{0,2,1:T(8,128)S(1)}, f32[128,20,112]{0,2,1:T(8,128)}, u32[]{:S(2)}) copy-start(f32[128,20,112]{0,2,1:T(8,128)} %copy.42) | copy-start | bytes 3440644
  163.5 3.4 %copy-start.34 = (f32[128,20]{0,1:T(8,128)S(1)}, f32[128,20]{0,1:T(8,128)}, u32[]{:S(2)}) copy-start(f32[128,20]{0,1:T(8,128)} %copy-done.33) | copy-start | bytes 30724
  163.6 3.4 %copy-start.35 = (f32[20,112]{1,0:T(8,128)S(1)}, f32[20,112]{1,0:T(8,128)}, u32[]{:S(2)}) copy-start(f32[20,112]{1,0:T(8,128)} %reshape.87) | copy-start | bytes 26884
  163.6 3.4 %copy-start.38 = (f32[128,20]{0,1:T(8,128)S(1)}, f32[128,20]{0,1:T(8,128)}, u32[]{:S(2)}) copy-start(f32[128,20]{0,1:T(8,128)} %copy-done.36) | copy-start | bytes 30724
  198.4 5.6 %copy-start.13 = (f32[10,112,112]{2,1,0:T(8,128)S(1)}, f32[10,112,112]{2,1,0:T(8,128)}, u32[]{:S(2)}) copy-start(f32[10,112,112]{2,1,0:T(8,128)} %reduce-scatter.9.cloned.1.call-done) | copy-start | bytes 1505284
  204.0 4.4 %copy-start.6 = (bf16[128,20,112]{0,2,1:T(8,128)(2,1)S(1)}, bf16[128,20,112]{0,2,1:T(8,128)(2,1)}, u32[]{:S(2)}) copy-start(bf16[128,20,112]{0,2,1:T(8,128)(2,1)} %copy-done.5) | copy-start | bytes 1720324
  206.5 3.4 %copy-start.8 = (bf16[128,20,112]{0,2,1:T(8,128)(2,1)S(1)}, bf16[128,20,112]{0,2,1:T(8,128)(2,1)}, u32[]{:S(2)}) copy-start(bf16[128,20,112]{0,2,1:T(8,128)(2,1)} %copy-done.7) | copy-start | bytes 1720324
  211.1 3.0 %copy-start.11 = (f32[128,20,112]{0,2,1:T(8,128)S(1)}, f32[128,20,112]{0,2,1:T(8,128)}, u32[]{:S(2)}) copy-start(f32[128,20,112]{0,2,1:T(8,128)} %convolution_bitcast_fusion) | copy-start | bytes 3440644
  215.7 1.9 copy-start.4
  217.6 2.9 %copy-start.2 = (bf16[1,4,32,2240]{3,2,1,0:T(8,128)(2,1)S(1)}, bf16[1,4,32,2240]{3,2,1,0:T(8,128)(2,1)}, u32[]{:S(2)}) copy-start(bf16[1,4,32,2240]{3,2,1,0:T(8,128)(2,1)} %param.12) | copy-start | bytes 1720324
  217.6 2.9 %copy-start.21 = (bf16[1,1,32,2240]{3,2,1,0:T(8,128)(2,1)S(1)}, bf16[1,1,32,2240]{3,2,1,0:T(8,128)(2,1)}, u32[]{:S(2)}) copy-start(bf16[1,1,32,2240]{3,2,1,0:T(8,128)(2,1)} %copy-done.20) | copy-start | bytes 430084
  217.6 2.9 %copy-start.23 = (f32[2240]{0:T(1024)S(1)}, f32[2240]{0:T(1024)}, u32[]{:S(2)}) copy-start(f32[2240]{0:T(1024)} %get-tuple-element.138) | copy-start | bytes 26884
  217.7 2.9 %copy-start.24 = (f32[2240]{0:T(1024)S(1)}, f32[2240]{0:T(1024)}, u32[]{:S(2)}) copy-start(f32[2240]{0:T(1024)} %get-tuple-element.139) | copy-start | bytes 26884
  217.7 2.9 %copy-start.25 = (f32[2240]{0:T(1024)S(1)}, f32[2240]{0:T(1024)}, u32[]{:S(2)}) copy-start(f32[2240]{0:T(1024)} %get-tuple-element.140) | copy-start | bytes 26884
  217.7 2.9 %copy-start.26 = (f32[2240]{0:T(1024)S(1)}, f32[2240]{0:T(1024)}, u32[]{:S(2)}) copy-start(f32[2240]{0:T(1024)} %get-tuple-element.141) | copy-start | bytes 26884
  217.7 2.9 %copy-start.27 = (f32[2240]{0:T(1024)S(1)}, f32[2240]{0:T(1024)}, u32[]{:S(2)}) copy-start(f32[2240]{0:T(1024)} %get-tuple-element.142) | copy-start | bytes 26884
  217.7 2.9 %copy-start.28 = (f32[2240]{0:T(1024)S(1)}, f32[2240]{0:T(1024)}, u32[]{:S(2)}) copy-start(f32[2240]{0:T(1024)} %get-tuple-element.143) | copy-start | bytes 26884
  217.7 2.9 %copy-start.29 = (f32[2240]{0:T(1024)S(1)}, f32[2240]{0:T(1024)}, u32[]{:S(2)}) copy-start(f32[2240]{0:T(1024)} %get-tuple-element.144) | copy-start | bytes 26884
  (3 other events, 3.0 us)
Sparse Core Ops, SparseCore 0:
  13.4 9.9 reduce-scatter.6
  25.6 78.6 all-gather.10
  112.5 13.7 reduce-scatter.8
  128.4 52.3 all-gather.12
Sparse Core Ops, SparseCore 1:
  141.7 104.1 all-reduce.7
where the time goes:
time: 256 us; the launch traced here: 255 us
  waiting for transfers between devices  86.4 us (34%)
  blocking collectives  71.2 us (28%)
  other arithmetic  27.1 us (11%)
  local copies, waits for them, and re-layouts  26.9 us (11%)
  between operations  16.6 us (6%)
  starting transfers between devices  14 us (5%)
  matrix products  12.1 us (5%)
    all_gather x1, waiting for transfers between devices, carried_in(): gathered = jax.tree.map(lambda a: lax.all_gather(a, axis), part)  39.8 us
    all_gather x1, blocking collectives, carried_in(): gathered = jax.tree.map(lambda a: lax.all_gather(a, axis), part)  28.8 us
    all_gather x1, blocking collectives, carried_in_2(): lax.all_gather(a.astype(kind), axis)  28 us
    psum x1, waiting for transfers between devices, shards(): taps_grad = lax.psum(jnp.stack(tap_rows), ('tm', 'space'))  22.5 us
    reduce_scatter x1, waiting for transfers between devices, shards(): lax.psum_scatter(grad_partial, 'space', scatter_dimension=0, tiled=True)  13.9 us
    reduce_scatter x1, waiting for transfers between devices, shards(): lax.psum_scatter(partial_value, 'space', scatter_dimension=0, tiled=True)  10.1 us
    add x14, other arithmetic, add_pair(): return (earlier[0] + later[0], earlier[1] + later[1])  7.9 us
    ppermute x2, starting transfers between devices, extended(): lax.ppermute(lax.slice_in_dim(block, block.shape[dim] - width, None, axis...  6.74 us
  transfers between devices with their start and end apart: 11, of which 4 were waited for; matrix products, arithmetic and copies ran while one was open for 22% of the time, Pallas kernels for 0%

commit v1 on v0

--- a/solution.py
+++ b/solution.py
@@ -161,7 +161,9 @@
             window = value_pad[:, row_off : row_off + row_count, col_off : col_off + col_count]
             tap_cols.append(jnp.sum(cotangent_full * window, axis=(0, 1, 2)))
         tap_rows.append(jnp.stack(tap_cols))
-    taps_grad = lax.psum(jnp.stack(tap_rows), ("tm", "space"))
+    value = jnp.stack(tap_rows)
+    parts = lax.all_gather(value, ("tm", "space"), axis=0, tiled=False)
+    taps_grad = parts.sum(axis=0)
     return (attended, query_grad, key_grad, value_grad, taps_grad)
 
 

time: 256 us -> 264 us (1.031)
  the two profiles are of different devices: /device:TPU:8 before, /device:TPU:0 now
where the time goes in v1:
time: 264 us; the launch traced here: 262 us
  waiting for transfers between devices  87.2 us (33%)
  blocking collectives  77.7 us (29%)
  other arithmetic  27.7 us (10%)
  local copies, waits for them, and re-layouts  25.9 us (10%)
  between operations  16.6 us (6%)
  starting transfers between devices  13.8 us (5%)
  matrix products  13.4 us (5%)
    all_gather x1, waiting for transfers between devices, carried_in(): gathered = jax.tree.map(lambda a: lax.all_gather(a, axis), part)  37.5 us
    all_gather x1, blocking collectives, carried_in(): gathered = jax.tree.map(lambda a: lax.all_gather(a, axis), part)  31.9 us
    all_gather x1, blocking collectives, carried_in_2(): lax.all_gather(a.astype(kind), axis)  31.1 us
    all_gather x1, waiting for transfers between devices, shards(): parts = lax.all_gather(value, ('tm', 'space'), axis=0, tiled=False)  29.7 us
    reduce_scatter x1, waiting for transfers between devices, shards(): lax.psum_scatter(partial_value, 'space', scatter_dimension=0, tiled=True)  11.3 us
    reduce_scatter x1, waiting for transfers between devices, shards(): lax.psum_scatter(grad_partial, 'space', scatter_dimension=0, tiled=True)  7.66 us
    add x14, other arithmetic, add_pair(): return (earlier[0] + later[0], earlier[1] + later[1])  7.58 us
    ppermute x2, starting transfers between devices, extended(): lax.ppermute(lax.slice_in_dim(block, block.shape[dim] - width, None, axis...  6.74 us
  transfers between devices with their start and end apart: 11, of which 5 were waited for; matrix products, arithmetic and copies ran while one was open for 15% of the time, Pallas kernels for 0%

profile of v1, /device:TPU:0, one launch (start us, length us, event | category | flops | bytes accessed | tf_op | source)
XLA Modules:
  0.0 262.4 jit_solution(17662649459920691666)
XLA Ops:
  8.0 1.1 broadcast_maximum_fusion.1
  12.6 1.5 fusion.43
  14.1 11.3 %reduce-scatter.7.cloned.1.call-done = f32[10,112,112]{2,1,0:T(8,128)} async-done(((f32[20,112,112]{2,1,0:T(8,128)}), f32[10,112,112]{2,1,0:T(8,128)}) %reduce-scatter.7.cloned.1.call-update) | async-done | bytes 501776 | tf_op jit(solution)/shard_map/reduce_scatter | solution.py:96
  25.7 2.8 %fusion = f32[16,112]{1,0:T(8,128)S(1)} fusion(f32[20,112]{1,0:T(8,128)S(1)} %reduce_sum.111), kind=kCustom, calls=%all-reduce-scatter | all-reduce-scatter fusion | flops 3585 | bytes 16640
  28.6 2.1 collective-permute-start.4
  31.5 1.5 copy.42
  34.2 1.7 reshape.72
  35.9 1.6 copy.40
  37.7 31.9 %all-gather.5 = f32[8,10,112]{2,1,0:T(8,128)S(1)} all-gather(f32[1,10,112]{2,1,0:T(8,128)S(1)} %fusion.37), channel_id=3, replica_groups=mesh['groups'=2,'tm'=8,'space'=2] {'tm'}, dimensions={0}, use_global_device_ids=true | all-gather | bytes 40320 | tf_op jit(solution)/shard_map/all_gather | solution.py:25
  69.6 37.5 %all-gather.13.cloned.1.call-done = f32[80,112,112]{2,1,0:T(8,128)} async-done(((f32[10,112,112]{2,1,0:T(8,128)}), f32[80,112,112]{2,1,0:T(8,128)}) %all-gather.13.cloned.1.call-update) | async-done | bytes 4014096 | tf_op jit(solution)/shard_map/all_gather | solution.py:25
  107.2 1.8 all-gather.6
  109.6 3.6 %fusion.33 = f32[20,112,112]{2,1,0:T(8,128)} fusion(bf16[128,20,112]{0,2,1:T(8,128)(2,1)S(1)} %copy.40, f32[128,20,112]{0,2,1:T(8,128)} %copy.42, f32[128,20]{0,1:T(8,128)S(1)} %fusion.34), kind=kOutput, calls=%fused_computation.74 | convolution fusion | flops 385638400 | bytes 2734080 | tf_op jit(solution)/shard_map/the,thd->hed/dot_general | solution.py:121
  113.3 1.3 collective-permute-start.1
  114.6 3.0 %collective-permute-start = (bf16[1,1,32,2240]{3,2,1,0:T(8,128)(2,1)S(1)}, bf16[1,1,32,2240]{3,2,1,0:T(8,128)(2,1)S(1)}, u32[]{:S(2)}, u32[]{:S(2)}) collective-permute-start(bf16[1,1,32,2240]{3,2,1,0:T(8,128)(2,1)S(1)} %get-tuple-element.171), channel_id=1, source_target_pairs={{0,1},{2,3},{4,5},{6,7},{8,9},{10,11},{12,13},{14,15},{16,17},{18,... | collective-permute-start | bytes 430088 | tf_op jit(solution)/shard_map/ppermute | solution.py:15
  119.0 1.1 fusion.23
  121.1 7.7 %reduce-scatter.9.cloned.1.call-done = f32[10,112,112]{2,1,0:T(8,128)} async-done(((f32[20,112,112]{2,1,0:T(8,128)}), f32[10,112,112]{2,1,0:T(8,128)}) %reduce-scatter.9.cloned.1.call-update) | async-done | bytes 501776 | tf_op jit(solution)/shard_map/reduce_scatter | solution.py:124
  128.8 1.8 convert_element_type.134
  130.7 1.3 collective-permute-start.3
  132.0 3.7 %collective-permute-start.2 = (bf16[1,1,32,2240]{3,2,1,0:T(8,128)(2,1)S(1)}, bf16[1,1,32,2240]{3,2,1,0:T(8,128)(2,1)}, u32[]{:S(2)}, u32[]{:S(2)}) collective-permute-start(bf16[1,1,32,2240]{3,2,1,0:T(8,128)(2,1)S(1)} %get-tuple-element.169), channel_id=1, source_target_pairs={{0,1},{2,3},{4,5},{6,7},{8,9},{10,11},{12,13},{14,15},{16,17},{18,... | collective-permute-start | bytes 430088 | tf_op jit(solution)/shard_map/ppermute | solution.py:15
  137.2 1.5 select_maximum_fusion
  138.7 29.7 %all-gather.17.cloned.1.call-done = f32[48,3,2240]{2,1,0:T(4,128)} async-done(((f32[3,3,2240]{2,1,0:T(4,128)}), f32[48,3,2240]{2,1,0:T(4,128)}) %all-gather.17.cloned.1.call-update) | async-done | bytes 1290256 | tf_op jit(solution)/shard_map/all_gather | solution.py:165
  168.4 2.4 reduce_sum.122
  171.4 1.1 add.143
  172.6 2.9 %all_gather.46 = f32[20,112,112]{2,1,0:T(8,128)S(1)} all-gather(f32[10,112,112]{2,1,0:T(8,128)S(1)} %add.143), channel_id=1, replica_groups=mesh['groups'=2,'tm'=8,'space'=2] {'space'}, dimensions={0}, use_global_device_ids=true | all-gather | bytes 1505280 | tf_op jit(solution)/shard_map/all_gather | solution.py:106
  175.5 2.7 %multiply_reduce_fusion = (f32[128,20]{0,1:T(8,128)}, f32[128,20,112]{0,2,1:T(8,128)}) fusion(f32[128,20,112]{0,2,1:T(8,128)S(1)} %copy-done.17, f32[128,20]{0,1:T(8,128)S(1)} %copy-done.37, f32[20,112,112]{2,1,0:T(8,128)S(1)} %all_gather.46, bf16[128,20,112]{0,2,1:T(8,128)(2,1)S(1)} %copy-done.10), kind=kOutput, calls=%fused_computation.62 | convolution fusion | flops 386209280 | bytes 3891200 | tf_op jit(solution)/shard_map/the,hed->thd/dot_general | solution.py:110
  178.2 2.9 %copy.41 = f32[128,20,112]{2,1,0:T(8,128)} copy(f32[128,20,112]{0,2,1:T(8,128)} %get-tuple-element.174) | data formatting | bytes 2293760 | tf_op jit(solution)/shard_map/div | solution.py:112
  181.2 2.7 %reshape.73 = f32[1,4,32,2240]{3,2,1,0:T(8,128)} reshape(f32[128,20,112]{2,1,0:T(8,128)} %copy.41) | data formatting | bytes 2293760 | tf_op jit(solution)/shard_map/reshape | solution.py:113
  185.6 2.7 %fusion.1 = f32[16,112]{1,0:T(8,128)S(1)} fusion(f32[20,112]{1,0:T(8,128)S(1)} %bitcast.90), kind=kCustom, calls=%all-reduce-scatter.1 | all-reduce-scatter fusion | flops 3585 | bytes 16640
  188.3 2.2 collective-permute-start.5
  190.6 3.3 %fusion.15 = bf16[1,4,32,2240]{3,2,1,0:T(8,128)(2,1)} fusion(f32[1,4,32,2240]{3,2,1,0:T(8,128)} %reshape.73, bf16[1,4,32,2240]{3,2,1,0:T(8,128)(2,1)S(1)} %copy-done, bf16[1,1,32,2240]{3,2,1,0:T(8,128)(2,1)S(1)} %collective-permute-done.1, bf16[1,1,32,2240]{3,2,1,0:T(8,128)(2,1)} %copy-done.14, f32[2240]{0:T(1024)} %get-tuple-element.143, ...), kind=kLoop, calls=%fused_computation.42 | loop fusion | flops 8601600 | bytes 6101760 | tf_op jit(solution)/shard_map/convert_element_type | solution.py:113
  193.9 1.4 fusion.5
  195.8 1.4 reshape.75
  197.4 31.1 %all-gather.7 = bf16[8,10,112]{2,1,0:T(8,128)(2,1)S(1)} all-gather(bf16[1,10,112]{2,1,0:T(8,128)(2,1)S(1)} %fusion.39), channel_id=5, replica_groups=mesh['groups'=2,'tm'=8,'space'=2] {'tm'}, dimensions={0}, use_global_device_ids=true | all-gather | bytes 20160 | tf_op jit(solution)/shard_map/all_gather | solution.py:41
  228.6 7.8 %while.27 = (s32[]{:T(128)}, f32[10,112,112]{2,1,0:T(8,128)S(1)}, f32[10,112]{1,0:T(8,128)S(1)}, s32[]{:T(128)}, bf16[8,10,112,112]{3,2,1,0:T(8,128)(2,1)}, /*in...) while((s32[]{:T(128)}, f32[10,112,112]{2,1,0:T(8,128)S(1)}, ...), condition=%wide.region_9.10_spmd, body=%wide.region_8.9_spmd.sunk | while | flops 253126 | bytes 1265763 | solution.py:56
  228.6 1.1 convert_add_fusion.4
  229.7 1.1 convert_add_fusion.4
  230.8 1.1 convert_add_fusion.4
  232.0 1.1 convert_add_fusion.4
  236.4 2.3 all_gather.52
  238.8 1.9 all-gather.8
  240.8 1.4 convolution_bitcast_fusion
  242.2 1.3 fusion.3
  243.4 1.5 copy.47
  244.9 1.4 reshape.76
  246.3 1.8 copy.50
  248.1 1.4 reshape.77
  249.6 2.9 %select_convert_fusion = (bf16[1,4,32,2240]{3,2,1,0:T(8,128)(2,1)}, bf16[1,4,32,2240]{3,2,1,0:T(8,128)(2,1)}) fusion(bf16[1,4,32,2240]{3,2,1,0:T(8,128)(2,1)} %reshape.76, bf16[1,4,32,2240]{3,2,1,0:T(8,128)(2,1)S(1)} %copy-done.4, bf16[1,4,32,2240]{3,2,1,0:T(8,128)(2,1)} %reshape.75, bf16[1,4,32,2240]{3,2,1,0:T(8,128)(2,1)} %param.9), kind=kLoop, calls=%fused_computation.59 | loop fusion | flops 2007040 | bytes 3440640 | tf_op jit(solution)/shard_map/convert_element_type | solution.py:151
  252.6 2.7 %fusion.22 = bf16[1,4,32,2240]{3,2,1,0:T(8,128)(2,1)} fusion(f32[1,4,32,2240]{3,2,1,0:T(8,128)S(1)} %copy-done.11, bf16[1,4,32,2240]{3,2,1,0:T(8,128)(2,1)S(1)} %copy-done.2, bf16[1,6,34,2240]{3,2,1,0:T(8,128)(2,1)S(1)} %select_maximum_fusion, bf16[1,1,32,2240]{3,2,1,0:T(8,128)(2,1)} %collective-permute-done.2, bf16[1,1,32,2240]{3,2,1,0:T(8,128)(2,1)S(1)} %copy-done.20, ...), kind=kLoop, calls=%fused_computation.49 | loop fusion | flops 8601600 | bytes 6101760 | tf_op jit(solution)/shard_map/convert_element_type | solution.py:153
  (155 shorter events, 16.2 us)
Async XLA Ops:
  8.0 17.4 %reduce-scatter.7.cloned.1.call-start = ((), (), s32[]{:S(2)}) async-start(), calls=%async_computation.2 | async-start | bytes 1720320 | tf_op jit(solution)/shard_map/reduce_scatter | solution.py:96
  9.2 1.3 copy-start
  10.5 1.3 copy-start.5
  14.1 11.4 %copy-start.3 = (bf16[1,4,32,2240]{3,2,1,0:T(8,128)(2,1)S(1)}, bf16[1,4,32,2240]{3,2,1,0:T(8,128)(2,1)}, u32[]{:S(2)}) copy-start(bf16[1,4,32,2240]{3,2,1,0:T(8,128)(2,1)} %param.10) | copy-start | bytes 1720324
  14.1 16.6 %copy-start.12 = (bf16[1,4,32,2240]{3,2,1,0:T(8,128)(2,1)S(1)}, bf16[1,4,32,2240]{3,2,1,0:T(8,128)(2,1)}, u32[]{:S(2)}) copy-start(bf16[1,4,32,2240]{3,2,1,0:T(8,128)(2,1)} %param.9) | copy-start | bytes 1720324
  14.1 93.0 %all-gather.13.cloned.1.call-start = ((), (), s32[]{:S(2)}) async-start(), calls=%async_computation.4 | async-start | bytes 5160960 | tf_op jit(solution)/shard_map/all_gather | solution.py:25
  25.4 5.3 %copy-start.1 = (bf16[1,4,32,2240]{3,2,1,0:T(8,128)(2,1)S(1)}, bf16[1,4,32,2240]{3,2,1,0:T(8,128)(2,1)}, u32[]{:S(2)}) copy-start(bf16[1,4,32,2240]{3,2,1,0:T(8,128)(2,1)} %param.12) | copy-start | bytes 1720324
  25.4 103.4 %reduce-scatter.9.cloned.1.call-start = ((), (), s32[]{:S(2)}) async-start(), calls=%async_computation.3 | async-start | bytes 1720320 | tf_op jit(solution)/shard_map/reduce_scatter | solution.py:124
  28.6 9.0 %collective-permute-start.4 = (f32[6,112]{1,0:T(8,128)S(1)}, f32[6,112]{1,0:T(8,128)S(1)}, u32[]{:S(2)}, u32[]{:S(2)}) collective-permute-start(f32[6,112]{1,0:T(8,128)S(1)} %slice.158), channel_id=1, source_target_pairs={{0,1},{2,3},{4,5},{6,7},{8,9},{10,11},{12,13},{14,15},{16,17},{18,... | collective-permute-start | bytes 8072
  31.5 1.5 copy-start.39
  37.5 72.1 %copy-start.9 = (bf16[128,20,112]{0,2,1:T(8,128)(2,1)}, bf16[128,20,112]{0,2,1:T(8,128)(2,1)S(1)}, u32[]{:S(2)}) copy-start(bf16[128,20,112]{0,2,1:T(8,128)(2,1)S(1)} %copy.40) | copy-start | bytes 1720324
  109.6 3.7 %copy-start.29 = (f32[20,1,128]{2,1,0:T(1,128)}, f32[20,1,128]{2,1,0:T(1,128)S(1)}, u32[]{:S(2)}) copy-start(f32[20,1,128]{2,1,0:T(1,128)S(1)} %fusion.44) | copy-start | bytes 30724
  109.6 3.6 %copy-start.36 = (f32[128,20]{0,1:T(8,128)}, f32[128,20]{0,1:T(8,128)S(1)}, u32[]{:S(2)}) copy-start(f32[128,20]{0,1:T(8,128)S(1)} %fusion.34) | copy-start | bytes 30724
  113.2 55.2 %all-gather.17.cloned.1.call-start = ((), (), s32[]{:S(2)}) async-start(), calls=%async_computation.6 | async-start | bytes 1880064 | tf_op jit(solution)/shard_map/all_gather | solution.py:165
  113.3 4.4 %collective-permute-start.1 = (bf16[1,1,32,2240]{3,2,1,0:T(8,128)(2,1)S(1)}, bf16[1,1,32,2240]{3,2,1,0:T(8,128)(2,1)S(1)}, u32[]{:S(2)}, u32[]{:S(2)}) collective-permute-start(bf16[1,1,32,2240]{3,2,1,0:T(8,128)(2,1)S(1)} %get-tuple-element.172), channel_id=1, source_target_pairs={{1,0},{3,2},{5,4},{7,6},{9,8},{11,10},{13,12},{15,14},{17,16},{19,... | collective-permute-start | bytes 430088 | tf_op jit(solution)/shard_map/ppermute | solution.py:18
  114.6 4.0 %collective-permute-start = (bf16[1,1,32,2240]{3,2,1,0:T(8,128)(2,1)S(1)}, bf16[1,1,32,2240]{3,2,1,0:T(8,128)(2,1)S(1)}, u32[]{:S(2)}, u32[]{:S(2)}) collective-permute-start(bf16[1,1,32,2240]{3,2,1,0:T(8,128)(2,1)S(1)} %get-tuple-element.171), channel_id=1, source_target_pairs={{0,1},{2,3},{4,5},{6,7},{8,9},{10,11},{12,13},{14,15},{16,17},{18,... | collective-permute-start | bytes 430088 | tf_op jit(solution)/shard_map/ppermute | solution.py:15
  118.7 1.5 copy-start.14
  120.2 15.5 %copy-start.30 = (f32[3,3,2240]{2,1,0:T(4,128)S(1)}, f32[3,3,2240]{2,1,0:T(4,128)}, u32[]{:S(2)}) copy-start(f32[3,3,2240]{2,1,0:T(4,128)} %param.13) | copy-start | bytes 241924
  121.1 107.4 %all-gather.15.cloned.1.call-start = ((), (), s32[]{:S(2)}) async-start(), calls=%async_computation.5 | async-start | bytes 2580480 | tf_op jit(solution)/shard_map/all_gather | solution.py:41
  130.7 5.8 %collective-permute-start.3 = (bf16[1,1,32,2240]{3,2,1,0:T(8,128)(2,1)S(1)}, bf16[1,1,32,2240]{3,2,1,0:T(8,128)(2,1)S(1)}, u32[]{:S(2)}, u32[]{:S(2)}) collective-permute-start(bf16[1,1,32,2240]{3,2,1,0:T(8,128)(2,1)S(1)} %get-tuple-element.170), channel_id=1, source_target_pairs={{1,0},{3,2},{5,4},{7,6},{9,8},{11,10},{13,12},{15,14},{17,16},{19,... | collective-permute-start | bytes 430088 | tf_op jit(solution)/shard_map/ppermute | solution.py:18
  132.0 5.2 %collective-permute-start.2 = (bf16[1,1,32,2240]{3,2,1,0:T(8,128)(2,1)S(1)}, bf16[1,1,32,2240]{3,2,1,0:T(8,128)(2,1)}, u32[]{:S(2)}, u32[]{:S(2)}) collective-permute-start(bf16[1,1,32,2240]{3,2,1,0:T(8,128)(2,1)S(1)} %get-tuple-element.169), channel_id=1, source_target_pairs={{0,1},{2,3},{4,5},{6,7},{8,9},{10,11},{12,13},{14,15},{16,17},{18,... | collective-permute-start | bytes 430088 | tf_op jit(solution)/shard_map/ppermute | solution.py:15
  171.4 4.1 %copy-start.37 = (f32[128,20]{0,1:T(8,128)S(1)}, f32[128,20]{0,1:T(8,128)}, u32[]{:S(2)}) copy-start(f32[128,20]{0,1:T(8,128)} %copy-done.36) | copy-start | bytes 30724
  172.5 3.0 %copy-start.10 = (bf16[128,20,112]{0,2,1:T(8,128)(2,1)S(1)}, bf16[128,20,112]{0,2,1:T(8,128)(2,1)}, u32[]{:S(2)}) copy-start(bf16[128,20,112]{0,2,1:T(8,128)(2,1)} %copy-done.9) | copy-start | bytes 1720324
  172.5 3.0 %copy-start.17 = (f32[128,20,112]{0,2,1:T(8,128)S(1)}, f32[128,20,112]{0,2,1:T(8,128)}, u32[]{:S(2)}) copy-start(f32[128,20,112]{0,2,1:T(8,128)} %copy.42) | copy-start | bytes 3440644
  175.5 2.7 %copy-start.15 = (f32[20,112,112]{2,1,0:T(8,128)}, f32[20,112,112]{2,1,0:T(8,128)S(1)}, u32[]{:S(2)}) copy-start(f32[20,112,112]{2,1,0:T(8,128)S(1)} %all_gather.46) | copy-start | bytes 3010564
  181.1 9.4 %copy-start.21 = (f32[2240]{0:T(1024)S(1)}, f32[2240]{0:T(1024)}, u32[]{:S(2)}) copy-start(f32[2240]{0:T(1024)} %get-tuple-element.137) | copy-start | bytes 26884
  188.3 5.6 %copy-start.31 = (f32[16,112]{1,0:T(8,128)}, f32[16,112]{1,0:T(8,128)S(1)}, u32[]{:S(2)}) copy-start(f32[16,112]{1,0:T(8,128)S(1)} %fusion.1) | copy-start | bytes 21508
  188.3 8.9 %collective-permute-start.5 = (f32[6,112]{1,0:T(8,128)S(1)}, f32[6,112]{1,0:T(8,128)S(1)}, u32[]{:S(2)}, u32[]{:S(2)}) collective-permute-start(f32[6,112]{1,0:T(8,128)S(1)} %slice.159), channel_id=1, source_target_pairs={{0,1},{2,3},{4,5},{6,7},{8,9},{10,11},{12,13},{14,15},{16,17},{18,... | collective-permute-start | bytes 8072
  190.5 3.4 %copy-start.16 = (f32[20,112,112]{2,1,0:T(8,128)S(1)}, f32[20,112,112]{2,1,0:T(8,128)}, u32[]{:S(2)}) copy-start(f32[20,112,112]{2,1,0:T(8,128)} %copy-done.15) | copy-start | bytes 3010564
  190.5 3.4 %copy-start.18 = (f32[128,20,112]{0,2,1:T(8,128)S(1)}, f32[128,20,112]{0,2,1:T(8,128)}, u32[]{:S(2)}) copy-start(f32[128,20,112]{0,2,1:T(8,128)} %copy.42) | copy-start | bytes 3440644
  190.5 3.4 %copy-start.34 = (f32[128,20]{0,1:T(8,128)S(1)}, f32[128,20]{0,1:T(8,128)}, u32[]{:S(2)}) copy-start(f32[128,20]{0,1:T(8,128)} %copy-done.33) | copy-start | bytes 30724
  190.6 3.4 %copy-start.35 = (f32[20,112]{1,0:T(8,128)S(1)}, f32[20,112]{1,0:T(8,128)}, u32[]{:S(2)}) copy-start(f32[20,112]{1,0:T(8,128)} %reshape.88) | copy-start | bytes 26884
  190.6 3.4 %copy-start.38 = (f32[128,20]{0,1:T(8,128)S(1)}, f32[128,20]{0,1:T(8,128)}, u32[]{:S(2)}) copy-start(f32[128,20]{0,1:T(8,128)} %copy-done.36) | copy-start | bytes 30724
  195.3 1.9 copy-start.32
  228.5 7.8 %copy-start.13 = (f32[10,112,112]{2,1,0:T(8,128)S(1)}, f32[10,112,112]{2,1,0:T(8,128)}, u32[]{:S(2)}) copy-start(f32[10,112,112]{2,1,0:T(8,128)} %reduce-scatter.9.cloned.1.call-done) | copy-start | bytes 1505284
  236.4 4.4 %copy-start.6 = (bf16[128,20,112]{0,2,1:T(8,128)(2,1)S(1)}, bf16[128,20,112]{0,2,1:T(8,128)(2,1)}, u32[]{:S(2)}) copy-start(bf16[128,20,112]{0,2,1:T(8,128)(2,1)} %copy-done.5) | copy-start | bytes 1720324
  238.8 3.4 %copy-start.8 = (bf16[128,20,112]{0,2,1:T(8,128)(2,1)S(1)}, bf16[128,20,112]{0,2,1:T(8,128)(2,1)}, u32[]{:S(2)}) copy-start(bf16[128,20,112]{0,2,1:T(8,128)(2,1)} %copy-done.7) | copy-start | bytes 1720324
  248.1 1.4 copy-start.4
  249.6 3.0 %copy-start.2 = (bf16[1,4,32,2240]{3,2,1,0:T(8,128)(2,1)S(1)}, bf16[1,4,32,2240]{3,2,1,0:T(8,128)(2,1)}, u32[]{:S(2)}) copy-start(bf16[1,4,32,2240]{3,2,1,0:T(8,128)(2,1)} %param.12) | copy-start | bytes 1720324
  249.6 3.0 %copy-start.11 = (f32[1,4,32,2240]{3,2,1,0:T(8,128)S(1)}, f32[1,4,32,2240]{3,2,1,0:T(8,128)}, u32[]{:S(2)}) copy-start(f32[1,4,32,2240]{3,2,1,0:T(8,128)} %reshape.77) | copy-start | bytes 3440644
  249.6 3.0 %copy-start.20 = (bf16[1,1,32,2240]{3,2,1,0:T(8,128)(2,1)S(1)}, bf16[1,1,32,2240]{3,2,1,0:T(8,128)(2,1)}, u32[]{:S(2)}) copy-start(bf16[1,1,32,2240]{3,2,1,0:T(8,128)(2,1)} %copy-done.19) | copy-start | bytes 430084
  249.6 3.0 %copy-start.22 = (f32[2240]{0:T(1024)S(1)}, f32[2240]{0:T(1024)}, u32[]{:S(2)}) copy-start(f32[2240]{0:T(1024)} %get-tuple-element.138) | copy-start | bytes 26884
  249.6 3.0 %copy-start.23 = (f32[2240]{0:T(1024)S(1)}, f32[2240]{0:T(1024)}, u32[]{:S(2)}) copy-start(f32[2240]{0:T(1024)} %get-tuple-element.139) | copy-start | bytes 26884
  249.6 3.0 %copy-start.24 = (f32[2240]{0:T(1024)S(1)}, f32[2240]{0:T(1024)}, u32[]{:S(2)}) copy-start(f32[2240]{0:T(1024)} %get-tuple-element.140) | copy-start | bytes 26884
  249.6 3.0 %copy-start.25 = (f32[2240]{0:T(1024)S(1)}, f32[2240]{0:T(1024)}, u32[]{:S(2)}) copy-start(f32[2240]{0:T(1024)} %get-tuple-element.141) | copy-start | bytes 26884
  249.6 3.0 %copy-start.26 = (f32[2240]{0:T(1024)S(1)}, f32[2240]{0:T(1024)}, u32[]{:S(2)}) copy-start(f32[2240]{0:T(1024)} %get-tuple-element.142) | copy-start | bytes 26884
  249.6 3.0 %copy-start.27 = (f32[2240]{0:T(1024)S(1)}, f32[2240]{0:T(1024)}, u32[]{:S(2)}) copy-start(f32[2240]{0:T(1024)} %get-tuple-element.143) | copy-start | bytes 26884
  249.6 3.0 %copy-start.28 = (f32[2240]{0:T(1024)S(1)}, f32[2240]{0:T(1024)}, u32[]{:S(2)}) copy-start(f32[2240]{0:T(1024)} %get-tuple-element.144) | copy-start | bytes 26884
  (3 other events, 2.5 us)
Sparse Core Ops, SparseCore 0:
  14.2 11.1 reduce-scatter.6
  27.6 79.4 all-gather.12
  113.4 15.3 reduce-scatter.8
Sparse Core Ops, SparseCore 1:
  121.2 47.2 all-gather.16
  170.5 50.2 all-gather.14
